TPU v7x, 128 devices: a whole 4x4x4 slice. The times are simulated.
128 devices in a mesh: dp: 8 (over x, core), fsdp: 16 (over z, y).
Axes of the slice: x: 4, y: 4, z: 4, core: 2. Of those that a mesh axis runs over, the one named last changes fastest.
Arguments:
- images: bfloat16 [256, 196, 512], P(('dp', 'fsdp')), may hold values from -6 to 6
- cotangent: bfloat16 [256, 196, 512], P(('dp', 'fsdp')), may hold values from -24 to 24
- counts: int32 [128], P(('dp', 'fsdp')), may hold values from 1 to 2, as said below
- rel_index: int32 [49, 49], replicated, may hold values from 0 to 168, as said below
- region_ids: int32 [196], replicated, may hold values from 0 to 8, as said below
- qkv_weight: bfloat16 [2, 512, 1536], P(None, 'fsdp'), may hold values from -0.25 to 0.25
- qv_bias: bfloat16 [2, 1024], P(None, 'fsdp'), may hold values from -3 to 3
- proj_weight: bfloat16 [2, 512, 512], P(None, 'fsdp'), may hold values from -1 to 1
- proj_bias: bfloat16 [2, 512], P(None, 'fsdp'), may hold values from -3 to 3
- fc1_weight: bfloat16 [2, 512, 2048], P(None, 'fsdp'), may hold values from -0.25 to 0.25
- fc1_bias: bfloat16 [2, 2048], P(None, 'fsdp'), may hold values from -3 to 3
- fc2_weight: bfloat16 [2, 2048, 512], P(None, 'fsdp'), may hold values from -0.125 to 0.125
- fc2_bias: bfloat16 [2, 512], P(None, 'fsdp'), may hold values from -3 to 3
- norm_gains: bfloat16 [2, 2, 512], P(None, None, 'fsdp'), may hold values from 0.5 to 1.5
- norm_biases: bfloat16 [2, 2, 512], P(None, None, 'fsdp'), may hold values from -3 to 3
- rel_table: bfloat16 [2, 169, 16], P(None, None, 'fsdp'), may hold values from -4 to 354
Outputs:
- activations: float32 [256, 196, 512], P(('dp', 'fsdp'))
- images_grad: float32 [256, 196, 512], P(('dp', 'fsdp'))
- qkv_weight_grad: float32 [2, 512, 1536], P(None, 'fsdp')
- qv_bias_grad: float32 [2, 1024], P(None, 'fsdp')
- proj_weight_grad: float32 [2, 512, 512], P(None, 'fsdp')
- proj_bias_grad: float32 [2, 512], P(None, 'fsdp')
- fc1_weight_grad: float32 [2, 512, 2048], P(None, 'fsdp')
- fc1_bias_grad: float32 [2, 2048], P(None, 'fsdp')
- fc2_weight_grad: float32 [2, 2048, 512], P(None, 'fsdp')
- fc2_bias_grad: float32 [2, 512], P(None, 'fsdp')
- norm_gains_grad: float32 [2, 2, 512], P(None, None, 'fsdp')
- norm_biases_grad: float32 [2, 2, 512], P(None, None, 'fsdp')
- rel_table_grad: float32 [2, 169, 16], P(None, None, 'fsdp')
Inputs may be any that keep to these rules, and one draw needn't show every extreme that they name: `counts`: 85 devices use all 2 slots, the others one; the used slots of a device come first. `rel_index`: entry (i, j) depends only on the offset between window positions i and j; distinct offsets have distinct entries. `region_ids`: nine rectangular regions of the shifted grid, separated by two row cuts and two column cuts; each id labels one region.
All inputs are finite; a program needn't handle non-finite values.
Results may differ from a plain program's by a relative error of at most 0.025.
Values may be sent and summed in bfloat16 or wider, within the bound.
No kernel may reach another device: no remote copies, remote signals or barrier semaphores. Data moves between devices by JAX's collectives and lax.ppermute only.
A program may use at most 192 MiB of HBM per device.

v0:
```python
import jax
import jax.numpy as jnp
from jax import lax
from jax.sharding import PartitionSpec as P

WINDOW = 7
SIDE = 14
SHIFT = 3
LAYERS = 2
TOKENS_IMG = 196
WIN_TOK = 49
TABLE = 169


EPS = 1e-05
MASKED = -1e30
INV_ROOT2 = 0.7071067811865476
INV_ROOT_2PI = 0.3989422804014327


def product(pattern, first_op, second_op):
    return jnp.einsum(pattern, first_op, second_op, preferred_element_type=jnp.float32)


def normalize(values, gain, offset):
    average = jnp.mean(values, -1, keepdims=True)
    centered = values - average
    inv_std = lax.rsqrt(jnp.mean(centered * centered, -1, keepdims=True) + EPS)
    unit_val = centered * inv_std
    return (unit_val * gain + offset, unit_val, inv_std)


def normalize_back(upstream, unit_val, inv_std, gain):
    d_unit = upstream * gain
    result = inv_std * (
        d_unit
        - jnp.mean(d_unit, -1, keepdims=True)
        - unit_val * jnp.mean(d_unit * unit_val, -1, keepdims=True)
    )
    return (result, jnp.sum(upstream * unit_val, 0), jnp.sum(upstream, 0))


def gelu_value(hidden):
    return 0.5 * hidden * (1.0 + jax.scipy.special.erf(hidden * INV_ROOT2))


def gelu_slope(hidden):
    return (
        0.5 * (1.0 + jax.scipy.special.erf(hidden * INV_ROOT2))
        + hidden * jnp.exp(-0.5 * hidden * hidden) * INV_ROOT_2PI
    )


def to_windows(tensor, shifted):
    n_images = tensor.shape[0]
    channels = tensor.shape[-1]
    per_side = SIDE // WINDOW
    grid_view = tensor.reshape(n_images, SIDE, SIDE, channels)
    if shifted:
        grid_view = jnp.roll(grid_view, (-SHIFT, -SHIFT), (1, 2))
    grid_view = grid_view.reshape(n_images, per_side, WINDOW, per_side, WINDOW, channels).transpose(
        0, 1, 3, 2, 4, 5
    )
    return grid_view.reshape(n_images * per_side * per_side, WIN_TOK, channels)


def from_windows(windows, shifted):
    per_side = SIDE // WINDOW
    n_images = windows.shape[0] // (per_side * per_side)
    channels = windows.shape[-1]
    grid_view = windows.reshape(n_images, per_side, per_side, WINDOW, WINDOW, channels).transpose(
        0, 1, 3, 2, 4, 5
    )
    grid_view = grid_view.reshape(n_images, SIDE, SIDE, channels)
    if shifted:
        grid_view = jnp.roll(grid_view, (SHIFT, SHIFT), (1, 2))
    return grid_view.reshape(n_images, TOKENS_IMG, channels)


def split_heads(tokens_f, shifted, n_heads):
    n_images = tokens_f.shape[0] // TOKENS_IMG
    windows = to_windows(tokens_f.reshape(n_images, TOKENS_IMG, -1), shifted)
    return windows.reshape(windows.shape[0], WIN_TOK, n_heads, -1)


def merge_heads(windows, shifted):
    merged = from_windows(windows.reshape(windows.shape[0], WIN_TOK, -1), shifted)
    return merged.reshape(-1, merged.shape[-1])


def masked_scores(query_win, key_win, pos_bias, allowed):
    scores = product("wqhd,wkhd->whqk", query_win, key_win) + pos_bias[None]
    if allowed is not None:
        per_image = allowed.shape[0]
        full_shape = scores.shape
        grouped = scores.reshape(
            full_shape[0] // per_image, per_image, full_shape[1], full_shape[2], full_shape[3]
        )
        scores = jnp.where(allowed[None, :, None], grouped, MASKED).reshape(full_shape)
    return scores


def layer_forward(tokens_f, weights, shifted, pos_bias, allowed):
    mix_w, mix_b, out_w, out_b, up_w, up_b, down_w, down_b, norm_gain, norm_shift, pos_table = (
        weights
    )
    feat_dim = mix_w.shape[0]
    n_heads = pos_table.shape[1]
    q_scale = (feat_dim // n_heads) ** (-0.5)
    gain_f = norm_gain.astype(jnp.float32)
    shift_f = norm_shift.astype(jnp.float32)
    normed, unit_one, rstd_one = normalize(tokens_f, gain_f[0], shift_f[0])
    normed_one = normed.astype(jnp.bfloat16)
    mixed_out = product("tc,cf->tf", normed_one, mix_w)
    bias_f = mix_b.astype(jnp.float32)
    queries = ((mixed_out[:, :feat_dim] + bias_f[:feat_dim]) * q_scale).astype(jnp.bfloat16)
    key_rows = mixed_out[:, feat_dim : 2 * feat_dim].astype(jnp.bfloat16)
    values = (mixed_out[:, 2 * feat_dim :] + bias_f[feat_dim:]).astype(jnp.bfloat16)
    query_win = split_heads(queries, shifted, n_heads)
    key_win = split_heads(key_rows, shifted, n_heads)
    value_win = split_heads(values, shifted, n_heads)
    scores = masked_scores(query_win, key_win, pos_bias, allowed)
    row_max = jnp.max(scores, -1, keepdims=True)
    log_total = row_max + jnp.log(jnp.sum(jnp.exp(scores - row_max), -1, keepdims=True))
    prob_bf = jnp.exp(scores - log_total).astype(jnp.bfloat16)
    attended = merge_heads(product("whqk,wkhd->wqhd", prob_bf, value_win), shifted).astype(
        jnp.bfloat16
    )
    residual = tokens_f + product("tc,ce->te", attended, out_w) + out_b.astype(jnp.float32)
    normed, unit_two, rstd_two = normalize(residual, gain_f[1], shift_f[1])
    normed_two = normed.astype(jnp.bfloat16)
    hidden = product("tc,cf->tf", normed_two, up_w) + up_b.astype(jnp.float32)
    act_bf = gelu_value(hidden).astype(jnp.bfloat16)
    result = residual + product("tf,fc->tc", act_bf, down_w) + down_b.astype(jnp.float32)
    saved = (
        unit_one,
        rstd_one,
        normed_one,
        query_win,
        key_win,
        value_win,
        log_total,
        attended,
        unit_two,
        rstd_two,
        normed_two,
        hidden,
        act_bf,
    )
    return (result, saved)


def layer_backward(gradient, saved, weights, shifted, pos_bias, allowed, fold_bias):
    mix_w, mix_b, out_w, out_b, up_w, up_b, down_w, down_b, norm_gain, norm_shift, pos_table = (
        weights
    )
    (
        unit_one,
        rstd_one,
        normed_one,
        query_win,
        key_win,
        value_win,
        log_total,
        attended,
        unit_two,
        rstd_two,
        normed_two,
        hidden,
        act_bf,
    ) = saved
    feat_dim = mix_w.shape[0]
    n_heads = pos_table.shape[1]
    q_scale = (feat_dim // n_heads) ** (-0.5)
    gain_f = norm_gain.astype(jnp.float32)
    down_b_grad = jnp.sum(gradient, 0)
    grad_bf = gradient.astype(jnp.bfloat16)
    grad_hidden = product("tc,fc->tf", grad_bf, down_w) * gelu_slope(hidden)
    up_b_grad = jnp.sum(grad_hidden, 0)
    hidden_bf = grad_hidden.astype(jnp.bfloat16)
    grad_normed = product("tf,cf->tc", hidden_bf, up_w)
    back_two, gain_two_grad, shift_two_grad = normalize_back(
        grad_normed, unit_two, rstd_two, gain_f[1]
    )
    grad_resid = gradient + back_two
    out_b_grad = jnp.sum(grad_resid, 0)
    resid_bf = grad_resid.astype(jnp.bfloat16)
    grad_attended = product("te,ce->tc", resid_bf, out_w).astype(jnp.bfloat16)
    attended_win = split_heads(grad_attended, shifted, n_heads)
    scores = masked_scores(query_win, key_win, pos_bias, allowed)
    attn_prob = jnp.exp(scores - log_total)
    grad_probs = product("wqhd,wkhd->whqk", attended_win, value_win)
    grad_values = product("whqk,wqhd->wkhd", attn_prob.astype(jnp.bfloat16), attended_win)
    grad_scores = attn_prob * (grad_probs - jnp.sum(attn_prob * grad_probs, -1, keepdims=True))
    table_grad = fold_bias(jnp.sum(grad_scores, 0))
    scores_bf = grad_scores.astype(jnp.bfloat16)
    grad_queries = merge_heads(product("whqk,wkhd->wqhd", scores_bf, key_win) * q_scale, shifted)
    grad_keys = merge_heads(product("whqk,wqhd->wkhd", scores_bf, query_win), shifted)
    grad_values = merge_heads(grad_values, shifted)
    mix_b_grad = jnp.concatenate([jnp.sum(grad_queries, 0), jnp.sum(grad_values, 0)])
    mixed_bf = jnp.concatenate([grad_queries, grad_keys, grad_values], -1).astype(jnp.bfloat16)
    grad_normed = product("tf,cf->tc", mixed_bf, mix_w)
    back_one, gain_one_grad, shift_one_grad = normalize_back(
        grad_normed, unit_one, rstd_one, gain_f[0]
    )
    factors = (
        (normed_one, mixed_bf),
        (attended, resid_bf),
        (normed_two, hidden_bf),
        (act_bf, grad_bf),
    )
    mix_w_grad = product("tc,tf->cf", normed_one, mixed_bf)
    out_w_grad = product("tc,te->ce", attended, resid_bf)
    up_w_grad = product("tc,tf->cf", normed_two, hidden_bf)
    down_w_grad = product("tf,tc->fc", act_bf, grad_bf)
    grads = (
        mix_w_grad,
        mix_b_grad,
        out_w_grad,
        out_b_grad,
        up_w_grad,
        up_b_grad,
        down_w_grad,
        down_b_grad,
        jnp.stack([gain_one_grad, gain_two_grad]),
        jnp.stack([shift_one_grad, shift_two_grad]),
        table_grad,
    )
    return (grad_resid + back_one, grads, factors)


def share_out(grads):
    return (
        lax.psum_scatter(
            grads[0].astype(jnp.bfloat16), "fsdp", scatter_dimension=0, tiled=True
        ).astype(jnp.float32),
        lax.psum_scatter(
            grads[1].astype(jnp.bfloat16), "fsdp", scatter_dimension=0, tiled=True
        ).astype(jnp.float32),
        lax.psum_scatter(
            grads[2].astype(jnp.bfloat16), "fsdp", scatter_dimension=0, tiled=True
        ).astype(jnp.float32),
        lax.psum_scatter(
            grads[3].astype(jnp.bfloat16), "fsdp", scatter_dimension=0, tiled=True
        ).astype(jnp.float32),
        lax.psum_scatter(
            grads[4].astype(jnp.bfloat16), "fsdp", scatter_dimension=0, tiled=True
        ).astype(jnp.float32),
        lax.psum_scatter(
            grads[5].astype(jnp.bfloat16), "fsdp", scatter_dimension=0, tiled=True
        ).astype(jnp.float32),
        lax.psum_scatter(
            grads[6].astype(jnp.bfloat16), "fsdp", scatter_dimension=0, tiled=True
        ).astype(jnp.float32),
        lax.psum_scatter(
            grads[7].astype(jnp.bfloat16), "fsdp", scatter_dimension=0, tiled=True
        ).astype(jnp.float32),
        lax.psum_scatter(
            grads[8].astype(jnp.bfloat16), "fsdp", scatter_dimension=1, tiled=True
        ).astype(jnp.float32),
        lax.psum_scatter(
            grads[9].astype(jnp.bfloat16), "fsdp", scatter_dimension=1, tiled=True
        ).astype(jnp.float32),
        lax.psum_scatter(
            grads[10].astype(jnp.bfloat16), "fsdp", scatter_dimension=1, tiled=True
        ).astype(jnp.float32),
    )


def sum_groups(shares):
    return (
        lax.psum(shares[0].astype(jnp.bfloat16), "dp").astype(jnp.float32),
        lax.psum(shares[1].astype(jnp.bfloat16), "dp").astype(jnp.float32),
        lax.psum(shares[2].astype(jnp.bfloat16), "dp").astype(jnp.float32),
        lax.psum(shares[3].astype(jnp.bfloat16), "dp").astype(jnp.float32),
        lax.psum(shares[4].astype(jnp.bfloat16), "dp").astype(jnp.float32),
        lax.psum(shares[5].astype(jnp.bfloat16), "dp").astype(jnp.float32),
        lax.psum(shares[6].astype(jnp.bfloat16), "dp").astype(jnp.float32),
        lax.psum(shares[7].astype(jnp.bfloat16), "dp").astype(jnp.float32),
        lax.psum(shares[8].astype(jnp.bfloat16), "dp").astype(jnp.float32),
        lax.psum(shares[9].astype(jnp.bfloat16), "dp").astype(jnp.float32),
        lax.psum(shares[10].astype(jnp.bfloat16), "dp").astype(jnp.float32),
    )


def on_device(
    images,
    cotangent,
    counts,
    rel_index,
    region_ids,
    qkv_weight,
    qv_bias,
    proj_weight,
    proj_bias,
    fc1_weight,
    fc1_bias,
    fc2_weight,
    fc2_bias,
    norm_gains,
    norm_biases,
    rel_table,
):
    n_images = images.shape[0]
    feat_dim = images.shape[2]
    live_mask = (jnp.arange(n_images) < counts[0]).astype(jnp.float32)[:, None, None]
    onehot = (rel_index.reshape(-1)[:, None] == jnp.arange(TABLE)[None, :]).astype(jnp.float32)
    ids_win = to_windows(region_ids.reshape(1, TOKENS_IMG, 1), False)[:, :, 0]
    allowed = ids_win[:, :, None] == ids_win[:, None, :]

    def fold_bias(grad_bias):
        flat_bias = grad_bias.transpose(1, 2, 0).reshape(WIN_TOK * WIN_TOK, -1)
        return jnp.einsum("pr,ph->rh", onehot, flat_bias, precision=lax.Precision.HIGHEST)

    tokens_f = images.astype(jnp.float32).reshape(-1, feat_dim)
    saved_all = []
    kept_all = []
    pos_biases = []
    for layer_id in range(LAYERS):
        weights = (
            lax.all_gather(qkv_weight[layer_id], "fsdp", axis=0, tiled=True),
            lax.all_gather(qv_bias[layer_id], "fsdp", axis=0, tiled=True),
            lax.all_gather(proj_weight[layer_id], "fsdp", axis=0, tiled=True),
            lax.all_gather(proj_bias[layer_id], "fsdp", axis=0, tiled=True),
            lax.all_gather(fc1_weight[layer_id], "fsdp", axis=0, tiled=True),
            lax.all_gather(fc1_bias[layer_id], "fsdp", axis=0, tiled=True),
            lax.all_gather(fc2_weight[layer_id], "fsdp", axis=0, tiled=True),
            lax.all_gather(fc2_bias[layer_id], "fsdp", axis=0, tiled=True),
            lax.all_gather(norm_gains[layer_id], "fsdp", axis=1, tiled=True),
            lax.all_gather(norm_biases[layer_id], "fsdp", axis=1, tiled=True),
            lax.all_gather(rel_table[layer_id], "fsdp", axis=1, tiled=True),
        )
        shifted = layer_id % 2 == 1
        gathered = jnp.einsum(
            "pr,rh->ph", onehot, weights[10].astype(jnp.float32), precision=lax.Precision.HIGHEST
        )
        pos_bias = gathered.reshape(WIN_TOK, WIN_TOK, -1).transpose(2, 0, 1)
        tokens_f, saved = layer_forward(
            tokens_f, weights, shifted, pos_bias, allowed if shifted else None
        )
        saved_all.append(saved)
        kept_all.append(weights)
        pos_biases.append(pos_bias)
    activations = tokens_f.reshape(n_images, TOKENS_IMG, feat_dim) * live_mask
    gradient = (cotangent.astype(jnp.float32) * live_mask).reshape(-1, feat_dim)
    totals_all = [None] * LAYERS
    for layer_id in reversed(range(LAYERS)):
        weights = (
            lax.all_gather(qkv_weight[layer_id], "fsdp", axis=0, tiled=True),
            lax.all_gather(qv_bias[layer_id], "fsdp", axis=0, tiled=True),
            lax.all_gather(proj_weight[layer_id], "fsdp", axis=0, tiled=True),
            lax.all_gather(proj_bias[layer_id], "fsdp", axis=0, tiled=True),
            lax.all_gather(fc1_weight[layer_id], "fsdp", axis=0, tiled=True),
            lax.all_gather(fc1_bias[layer_id], "fsdp", axis=0, tiled=True),
            lax.all_gather(fc2_weight[layer_id], "fsdp", axis=0, tiled=True),
            lax.all_gather(fc2_bias[layer_id], "fsdp", axis=0, tiled=True),
            lax.all_gather(norm_gains[layer_id], "fsdp", axis=1, tiled=True),
            lax.all_gather(norm_biases[layer_id], "fsdp", axis=1, tiled=True),
            lax.all_gather(rel_table[layer_id], "fsdp", axis=1, tiled=True),
        )
        shifted = layer_id % 2 == 1
        gradient, grads, factors = layer_backward(
            gradient,
            saved_all[layer_id],
            weights,
            shifted,
            pos_biases[layer_id],
            allowed if shifted else None,
            fold_bias,
        )
        shares = share_out(grads)
        totals_all[layer_id] = sum_groups(shares)
    stacked = [
        jnp.stack([totals_all[layer_id][member] for layer_id in range(LAYERS)])
        for member in range(11)
    ]
    return (
        activations,
        gradient.reshape(n_images, TOKENS_IMG, feat_dim),
        stacked[0],
        stacked[1],
        stacked[2],
        stacked[3],
        stacked[4],
        stacked[5],
        stacked[6],
        stacked[7],
        stacked[8],
        stacked[9],
        stacked[10],
    )


def solution(mesh):
    return jax.shard_map(
        on_device,
        mesh=mesh,
        in_specs=(
            P(("dp", "fsdp"), None, None),
            P(("dp", "fsdp"), None, None),
            P(("dp", "fsdp")),
            P(),
            P(),
            P(None, "fsdp", None),
            P(None, "fsdp"),
            P(None, "fsdp", None),
            P(None, "fsdp"),
            P(None, "fsdp", None),
            P(None, "fsdp"),
            P(None, "fsdp", None),
            P(None, "fsdp"),
            P(None, None, "fsdp"),
            P(None, None, "fsdp"),
            P(None, None, "fsdp"),
        ),
        out_specs=(
            P(("dp", "fsdp"), None, None),
            P(("dp", "fsdp"), None, None),
            P(None, "fsdp", None),
            P(None, "fsdp"),
            P(None, "fsdp", None),
            P(None, "fsdp"),
            P(None, "fsdp", None),
            P(None, "fsdp"),
            P(None, "fsdp", None),
            P(None, "fsdp"),
            P(None, None, "fsdp"),
            P(None, None, "fsdp"),
            P(None, None, "fsdp"),
        ),
        check_vma=False,
    )
```

profile of v0, /device:TPU:0, one launch (start us, length us, event | category | flops | bytes accessed | tf_op | source)
XLA Modules:
  0.0 1597.0 jit_solution(7504365914497293398)
XLA Ops:
  21.3 42.8 %all-reduce.17 = (bf16[1024]{0:T(1024)(128)(2,1)S(1)}, bf16[512]{0:T(512)(128)(2,1)S(1)}, bf16[512]{0:T(512)(128)(2,1)S(1)}, bf16[1024]{0:T(1024)(128)(2,1)S(1)}, bf16[512]{0:T(512)(128)(2,1)S(1)}) all-reduce(bf16[1024]{0:T(1024)(128)(2,1)S(1)} %dynamic-update-slice, ...), channel_id=5, replica_groups=mesh['dp'=8,'fsdp'=16] {'fsdp'}, use_global_device_ids=true, to_apply=%add | all-reduce | flops 3584 | bytes 14336
  65.3 17.0 %all-gather.19 = bf16[1,2048]{1,0:T(2,128)(2,1)S(1)} all-gather(bf16[1,128]{1,0:T(2,128)(2,1)S(1)} %get-tuple-element.182), channel_id=21, replica_groups=mesh['dp'=8,'fsdp'=16] {'fsdp'}, dimensions={1}, use_global_device_ids=true | all-gather | bytes 4352 | tf_op jit(solution)/shard_map/all_gather | solution.py:326
  82.9 20.6 %all-gather.8 = bf16[1,2048]{1,0:T(2,128)(2,1)S(1)} all-gather(bf16[1,128]{1,0:T(2,128)(2,1)S(1)} %get-tuple-element.183), channel_id=10, replica_groups=mesh['dp'=8,'fsdp'=16] {'fsdp'}, dimensions={1}, use_global_device_ids=true | all-gather | bytes 4352 | tf_op jit(solution)/shard_map/all_gather | solution.py:326
  103.9 21.0 %all-gather.15 = bf16[1,169,16]{1,0,2:T(2,128)(2,1)S(1)} all-gather(bf16[1,169,1]{1,0,2:T(2,128)(2,1)S(1)} %get-tuple-element.172), channel_id=17, replica_groups=mesh['dp'=8,'fsdp'=16] {'fsdp'}, dimensions={2}, use_global_device_ids=true | all-gather | bytes 5746 | tf_op jit(solution)/shard_map/all_gather | solution.py:331
  125.1 23.1 %all-gather.4 = bf16[1,169,16]{1,0,2:T(2,128)(2,1)S(1)} all-gather(bf16[1,169,1]{1,0,2:T(2,128)(2,1)S(1)} %get-tuple-element.173), channel_id=6, replica_groups=mesh['dp'=8,'fsdp'=16] {'fsdp'}, dimensions={2}, use_global_device_ids=true | all-gather | bytes 5746 | tf_op jit(solution)/shard_map/all_gather | solution.py:331
  150.5 21.3 %all-gather = bf16[1,2,512]{1,0,2:T(2,128)(2,1)S(1)} all-gather(bf16[1,2,32]{1,0,2:T(2,128)(2,1)S(1)} %copy.349), channel_id=2, replica_groups=mesh['dp'=8,'fsdp'=16] {'fsdp'}, dimensions={2}, use_global_device_ids=true | all-gather | bytes 2176 | tf_op jit(solution)/shard_map/all_gather | solution.py:329
  174.9 23.8 %all-gather.1 = bf16[1,2,512]{1,0,2:T(2,128)(2,1)S(1)} all-gather(bf16[1,2,32]{1,0,2:T(2,128)(2,1)S(1)} %copy.350), channel_id=3, replica_groups=mesh['dp'=8,'fsdp'=16] {'fsdp'}, dimensions={2}, use_global_device_ids=true | all-gather | bytes 2176 | tf_op jit(solution)/shard_map/all_gather | solution.py:330
  201.7 21.5 %all-gather.11 = bf16[1,2,512]{1,0,2:T(2,128)(2,1)S(1)} all-gather(bf16[1,2,32]{1,0,2:T(2,128)(2,1)S(1)} %copy.351), channel_id=13, replica_groups=mesh['dp'=8,'fsdp'=16] {'fsdp'}, dimensions={2}, use_global_device_ids=true | all-gather | bytes 2176 | tf_op jit(solution)/shard_map/all_gather | solution.py:329
  226.9 23.4 %all-gather.12 = bf16[1,2,512]{1,0,2:T(2,128)(2,1)S(1)} all-gather(bf16[1,2,32]{1,0,2:T(2,128)(2,1)S(1)} %copy.352), channel_id=14, replica_groups=mesh['dp'=8,'fsdp'=16] {'fsdp'}, dimensions={2}, use_global_device_ids=true | all-gather | bytes 2176 | tf_op jit(solution)/shard_map/all_gather | solution.py:330
  254.8 24.5 %all-gather.16 = bf16[1,512,512]{2,1,0:T(8,128)(2,1)} all-gather(bf16[1,32,512]{2,1,0:T(8,128)(2,1)S(1)} %get-tuple-element.166), channel_id=18, replica_groups=mesh['dp'=8,'fsdp'=16] {'fsdp'}, dimensions={1}, use_global_device_ids=true | all-gather | bytes 557056 | tf_op jit(solution)/shard_map/all_gather | solution.py:323
  279.2 23.0 %all-gather.5 = bf16[1,512,512]{2,1,0:T(8,128)(2,1)S(1)} all-gather(bf16[1,32,512]{2,1,0:T(8,128)(2,1)S(1)} %get-tuple-element.167), channel_id=7, replica_groups=mesh['dp'=8,'fsdp'=16] {'fsdp'}, dimensions={1}, use_global_device_ids=true | all-gather | bytes 557056 | tf_op jit(solution)/shard_map/all_gather | solution.py:323
  351.0 4.8 multiply_convert_fusion.1
  414.6 5.2 multiply_convert_fusion
  419.9 5.3 fusion.127
  448.3 4.8 convolution_bitcast_fusion
  453.2 4.9 copy.309
  475.2 4.6 copy.304
  484.6 4.9 copy.299
  592.9 72.1 %all-reduce.16 = (bf16[512]{0:T(512)(128)(2,1)S(1)}, bf16[1024]{0:T(1024)(128)(2,1)S(1)}, bf16[1024]{0:T(1024)(128)(2,1)S(1)}, bf16[512]{0:T(512)(128)(2,1)S(1)}...) all-reduce(bf16[512]{0:T(512)(128)(2,1)S(1)} %copy-done.99, ...), channel_id=23, replica_groups=mesh['dp'=8,'fsdp'=16] {'fsdp'}, use_global_device_ids=true, to_apply=%add.5 | all-reduce | flops 14112 | bytes 56448
  673.3 16.1 %reduce-scatter.39.cloned.1.call-done = bf16[32,2]{1,0:T(8,128)(2,1)} async-done(((bf16[512,2]{1,0:T(8,128)(2,1)}), bf16[32,2]{1,0:T(8,128)(2,1)}) %reduce-scatter.39.cloned.1.call-update) | async-done | bytes 144
  690.7 74.6 %reduce-scatter.41.cloned.1.call-done = bf16[32,2]{1,0:T(8,128)(2,1)} async-done(((bf16[512,2]{1,0:T(8,128)(2,1)}), bf16[32,2]{1,0:T(8,128)(2,1)}) %reduce-scatter.41.cloned.1.call-update) | async-done | bytes 144
  766.6 74.4 %reduce-scatter.37.cloned.1.call-done = bf16[32,2]{1,0:T(8,128)(2,1)} async-done(((bf16[512,2]{1,0:T(8,128)(2,1)}), bf16[32,2]{1,0:T(8,128)(2,1)}) %reduce-scatter.37.cloned.1.call-update) | async-done | bytes 144
  842.2 75.4 %reduce-scatter.27.cloned.1.call-done = bf16[32,512]{1,0:T(8,128)(2,1)} async-done(((bf16[512,512]{1,0:T(8,128)(2,1)}), bf16[32,512]{1,0:T(8,128)(2,1)}) %reduce-scatter.27.cloned.1.call-update) | async-done | bytes 32784 | tf_op jit(solution)/shard_map/reduce_scatter | solution.py:240
  917.7 76.5 %reduce-scatter.25.cloned.1.call-done = bf16[32,512]{1,0:T(8,128)(2,1)} async-done(((bf16[512,512]{1,0:T(8,128)(2,1)}), bf16[32,512]{1,0:T(8,128)(2,1)}) %reduce-scatter.25.cloned.1.call-update) | async-done | bytes 32784 | tf_op jit(solution)/shard_map/reduce_scatter | solution.py:240
  1028.4 26.7 %all-reduce.23.cloned.1.call-done = (bf16[1,64]{1,0:T(2,128)(2,1)}, bf16[1,64]{1,0:T(2,128)(2,1)}, bf16[1,32,512]{2,1,0:T(8,128)(2,1)}, bf16[1,32,512]{2,1,0:T(8...) async-done(((bf16[1,64]{1,0:T(2,128)(2,1)}, ...) | async-done | bytes 67764 | tf_op jit(solution)/shard_map/psum | solution.py:273
  1060.0 72.6 %reduce-scatter.23.cloned.1.call-done = bf16[32,1536]{1,0:T(8,128)(2,1)} async-done(((bf16[512,1536]{1,0:T(8,128)(2,1)}), bf16[32,1536]{1,0:T(8,128)(2,1)}) %reduce-scatter.23.cloned.1.call-update) | async-done | bytes 98320 | tf_op jit(solution)/shard_map/reduce_scatter | solution.py:234
  1132.6 77.1 %reduce-scatter.21.cloned.1.call-done = bf16[32,1536]{1,0:T(8,128)(2,1)} async-done(((bf16[512,1536]{1,0:T(8,128)(2,1)}), bf16[32,1536]{1,0:T(8,128)(2,1)}) %reduce-scatter.21.cloned.1.call-update) | async-done | bytes 98320 | tf_op jit(solution)/shard_map/reduce_scatter | solution.py:234
  1209.6 77.8 %reduce-scatter.31.cloned.1.call-done = bf16[32,2048]{1,0:T(8,128)(2,1)} async-done(((bf16[512,2048]{1,0:T(8,128)(2,1)}), bf16[32,2048]{1,0:T(8,128)(2,1)}) %reduce-scatter.31.cloned.1.call-update) | async-done | bytes 131088 | tf_op jit(solution)/shard_map/reduce_scatter | solution.py:246
  1287.4 77.8 %reduce-scatter.35.cloned.1.call-done = bf16[128,512]{1,0:T(8,128)(2,1)} async-done(((bf16[2048,512]{1,0:T(8,128)(2,1)}), bf16[128,512]{1,0:T(8,128)(2,1)}) %reduce-scatter.35.cloned.1.call-update) | async-done | bytes 131088 | tf_op jit(solution)/shard_map/reduce_scatter | solution.py:252
  1365.2 77.7 %reduce-scatter.33.cloned.1.call-done = bf16[128,512]{1,0:T(8,128)(2,1)} async-done(((bf16[2048,512]{1,0:T(8,128)(2,1)}), bf16[128,512]{1,0:T(8,128)(2,1)}) %reduce-scatter.33.cloned.1.call-update) | async-done | bytes 131088 | tf_op jit(solution)/shard_map/reduce_scatter | solution.py:252
  1442.9 77.8 %reduce-scatter.29.cloned.1.call-done = bf16[32,2048]{1,0:T(8,128)(2,1)} async-done(((bf16[512,2048]{1,0:T(8,128)(2,1)}), bf16[32,2048]{1,0:T(8,128)(2,1)}) %reduce-scatter.29.cloned.1.call-update) | async-done | bytes 131088 | tf_op jit(solution)/shard_map/reduce_scatter | solution.py:246
  1525.9 58.5 %all-reduce.25.cloned.1.call-done = (bf16[1,32,1536]{2,1,0:T(8,128)(2,1)}, bf16[1,32,1536]{2,1,0:T(8,128)(2,1)}, bf16[1,32,2048]{2,1,0:T(8,128)(2,1)}, bf16[1,32...) async-done(((bf16[1,32,1536]{2,1,0:T(8,128)(2,1)}, bf16[1,32,1536]{2,1,0:T(8,128)(2,1)}, bf16[1,32,2048]{2,1,0:T(8,128)(2,1)}, ...) | async-done | bytes 720912 | tf_op jit(solution)/shard_map/psum | solution.py:272
  (572 shorter events, 345.0 us)
Async XLA Ops:
  7.3 298.5 %all-gather.29.cloned.1.call-start = ((), (), s32[]{:S(2)}) async-start(), calls=%async_computation.20 | async-start | bytes 1671168 | tf_op jit(solution)/shard_map/all_gather | solution.py:321
  9.0 94.7 %copy-start.102 = (s32[196]{0:T(256)S(1)}, s32[196]{0:T(256)}, u32[]{:S(2)}) copy-start(s32[196]{0:T(256)} %param.20) | copy-start | bytes 2356
  9.0 140.1 %copy-start.48 = (bf16[2,32,512]{2,1,0:T(8,128)(2,1)S(1)}, bf16[2,32,512]{2,1,0:T(8,128)(2,1)}, u32[]{:S(2)}) copy-start(bf16[2,32,512]{2,1,0:T(8,128)(2,1)} %param.23) | copy-start | bytes 196612
  9.0 341.9 %all-gather.31.cloned.1.call-start = ((), (), s32[]{:S(2)}) async-start(), calls=%async_computation.21 | async-start | bytes 2228224 | tf_op jit(solution)/shard_map/all_gather | solution.py:325
  10.7 345.0 %all-gather.33.cloned.1.call-start = ((), (), s32[]{:S(2)}) async-start(), calls=%async_computation.22 | async-start | bytes 2228224 | tf_op jit(solution)/shard_map/all_gather | solution.py:327
  12.5 346.7 %all-gather.35.cloned.1.call-start = ((), (), s32[]{:S(2)}) async-start(), calls=%async_computation.23 | async-start | bytes 1671168 | tf_op jit(solution)/shard_map/all_gather | solution.py:321
  13.1 401.5 %all-gather.37.cloned.1.call-start = ((), (), s32[]{:S(2)}) async-start(), calls=%async_computation.24 | async-start | bytes 2228224 | tf_op jit(solution)/shard_map/all_gather | solution.py:325
  13.7 406.2 %all-gather.39.cloned.1.call-start = ((), (), s32[]{:S(2)}) async-start(), calls=%async_computation.25 | async-start | bytes 2228224 | tf_op jit(solution)/shard_map/all_gather | solution.py:327
  14.3 657.7 %reduce-scatter.43.cloned.1.call-start = ((), (), s32[]{:S(2)}) async-start(), calls=%async_computation.29 | async-start | bytes 139264
  16.4 285.9 %copy-start.83 = (f32[2]{0:T(128)}, f32[2]{0:T(128)S(1)}, u32[]{:S(2)}) copy-start(f32[2]{0:T(128)S(1)} %compare_convert_fusion) | copy-start | bytes 28
  103.7 119.6 %copy-start.60 = (s32[2401]{0:T(1024)}, s32[2401]{0:T(1024)S(1)}, u32[]{:S(2)}) copy-start(s32[2401]{0:T(1024)S(1)} %eq.34) | copy-start | bytes 28816
  149.3 156.4 %copy-start.44 = (f32[392]{0:T(512)}, f32[392]{0:T(512)S(1)}, u32[]{:S(2)}) copy-start(f32[392]{0:T(512)S(1)} %rsqrt.36) | copy-start | bytes 4708
  174.9 130.9 %copy-start.49 = (f32[512]{0:T(512)}, f32[512]{0:T(512)S(1)}, u32[]{:S(2)}) copy-start(f32[512]{0:T(512)S(1)} %get-tuple-element.99) | copy-start | bytes 6148
  174.9 176.1 %copy-start.66 = (f32[512]{0:T(512)}, f32[512]{0:T(512)S(1)}, u32[]{:S(2)}) copy-start(f32[512]{0:T(512)S(1)} %get-tuple-element.98) | copy-start | bytes 6148
  201.7 104.1 %copy-start.56 = (f32[512]{0:T(512)}, f32[512]{0:T(512)S(1)}, u32[]{:S(2)}) copy-start(f32[512]{0:T(512)S(1)} %get-tuple-element.101) | copy-start | bytes 6148
  201.7 149.2 %copy-start.85 = (f32[512]{0:T(512)}, f32[512]{0:T(512)S(1)}, u32[]{:S(2)}) copy-start(f32[512]{0:T(512)S(1)} %get-tuple-element.100) | copy-start | bytes 6148
  226.9 132.4 %copy-start.51 = (f32[512]{0:T(512)}, f32[512]{0:T(512)S(1)}, u32[]{:S(2)}) copy-start(f32[512]{0:T(512)S(1)} %get-tuple-element.95) | copy-start | bytes 6148
  253.8 105.5 %copy-start.58 = (f32[512]{0:T(512)}, f32[512]{0:T(512)S(1)}, u32[]{:S(2)}) copy-start(f32[512]{0:T(512)S(1)} %get-tuple-element.97) | copy-start | bytes 6148
  540.9 148.4 %reduce-scatter.39.cloned.1.call-start = ((), (), s32[]{:S(2)}) async-start(), calls=%async_computation.27 | async-start | bytes 139264
  578.9 186.3 %reduce-scatter.41.cloned.1.call-start = ((), (), s32[]{:S(2)}) async-start(), calls=%async_computation.28 | async-start | bytes 139264
  579.8 261.1 %reduce-scatter.37.cloned.1.call-start = ((), (), s32[]{:S(2)}) async-start(), calls=%async_computation.26 | async-start | bytes 139264
  581.1 336.6 %reduce-scatter.27.cloned.1.call-start = ((), (), s32[]{:S(2)}) async-start(), calls=%async_computation.15 | async-start | bytes 557056 | tf_op jit(solution)/shard_map/reduce_scatter | solution.py:240
  587.6 406.6 %copy-start.59 = (f32[512]{0:T(512)S(1)}, f32[512]{0:T(512)}, u32[]{:S(2)}) copy-start(f32[512]{0:T(512)} %copy-done.58) | copy-start | bytes 6148
  588.6 405.6 %reduce-scatter.25.cloned.1.call-start = ((), (), s32[]{:S(2)}) async-start(), calls=%async_computation.14 | async-start | bytes 557056 | tf_op jit(solution)/shard_map/reduce_scatter | solution.py:240
  592.8 462.4 %all-reduce.23.cloned.1.call-start = ((), (), s32[]{:S(2)}) async-start(), calls=%async_computation.30 | async-start | bytes 147456 | tf_op jit(solution)/shard_map/psum | solution.py:273
  994.2 138.3 %reduce-scatter.23.cloned.1.call-start = ((), (), s32[]{:S(2)}) async-start(), calls=%async_computation.13 | async-start | bytes 1671168 | tf_op jit(solution)/shard_map/reduce_scatter | solution.py:234
  997.9 211.7 %reduce-scatter.21.cloned.1.call-start = ((), (), s32[]{:S(2)}) async-start(), calls=%async_computation.12 | async-start | bytes 1671168 | tf_op jit(solution)/shard_map/reduce_scatter | solution.py:234
  1001.6 285.8 %reduce-scatter.31.cloned.1.call-start = ((), (), s32[]{:S(2)}) async-start(), calls=%async_computation.17 | async-start | bytes 2228224 | tf_op jit(solution)/shard_map/reduce_scatter | solution.py:246
  1005.9 359.3 %reduce-scatter.35.cloned.1.call-start = ((), (), s32[]{:S(2)}) async-start(), calls=%async_computation.19 | async-start | bytes 2228224 | tf_op jit(solution)/shard_map/reduce_scatter | solution.py:252
  1010.3 432.6 %reduce-scatter.33.cloned.1.call-start = ((), (), s32[]{:S(2)}) async-start(), calls=%async_computation.18 | async-start | bytes 2228224 | tf_op jit(solution)/shard_map/reduce_scatter | solution.py:252
  1014.7 506.0 %reduce-scatter.29.cloned.1.call-start = ((), (), s32[]{:S(2)}) async-start(), calls=%async_computation.16 | async-start | bytes 2228224 | tf_op jit(solution)/shard_map/reduce_scatter | solution.py:246
  1019.0 565.4 %all-reduce.25.cloned.1.call-start = ((), (), s32[]{:S(2)}) async-start(), calls=%async_computation.31 | async-start | bytes 1441792 | tf_op jit(solution)/shard_map/psum | solution.py:272
  (97 other events, 625.9 us)
Sparse Core Ops, SparseCore 0:
  10.8 46.3 all-gather.28
  59.9 44.2 all-gather.30
  106.4 44.5 all-gather.32
  152.9 43.1 all-gather.34
  198.7 44.8 all-gather.36
  245.6 44.0 all-gather.38
  541.1 71.8 reduce-scatter.42
  616.7 72.6 reduce-scatter.38
  692.6 72.6 reduce-scatter.40
  768.3 72.6 reduce-scatter.36
  844.7 72.8 reduce-scatter.26
  921.3 72.8 reduce-scatter.24
  998.7 56.3 all-reduce.22
  1058.2 74.3 reduce-scatter.22
  1135.6 73.9 reduce-scatter.20
  1212.8 74.6 reduce-scatter.30
  1290.5 74.6 reduce-scatter.34
  1368.3 74.5 reduce-scatter.32
  1446.2 74.4 reduce-scatter.28
  1523.3 61.0 all-reduce.24
where the time goes:
time: 1610 us; the launch traced here: 1600 us
  waiting for transfers between devices  865 us (54%)
  blocking collectives  334 us (21%)
  local copies, waits for them, and re-layouts  211 us (13%)
  matrix products  109 us (7%)
  other arithmetic  56.3 us (3%)
  between operations  20.5 us (1%)
    unnamed x24, waiting for transfers between devices  167 us
    reduce_scatter x2, waiting for transfers between devices, share_out(): lax.psum_scatter(grads[4].astype(jnp.bfloat16), 'fsdp', scatter_dimension...  156 us
    reduce_scatter x2, waiting for transfers between devices, share_out(): lax.psum_scatter(grads[6].astype(jnp.bfloat16), 'fsdp', scatter_dimension...  156 us
    reduce_scatter x2, waiting for transfers between devices, share_out(): lax.psum_scatter(grads[2].astype(jnp.bfloat16), 'fsdp', scatter_dimension...  152 us
    reduce_scatter x2, waiting for transfers between devices, share_out(): lax.psum_scatter(grads[0].astype(jnp.bfloat16), 'fsdp', scatter_dimension...  150 us
    unnamed x2, blocking collectives  115 us
    dot_general x36, matrix products, product(): jnp.einsum(pattern, first_op, second_op, preferred_element_type=jnp.float32)  105 us
    psum x1, waiting for transfers between devices, sum_groups(): lax.psum(shares[0].astype(jnp.bfloat16), 'dp').astype(jnp.float32)  58.5 us
  transfers between devices with their start and end apart: 20, of which 13 were waited for; matrix products, arithmetic and copies ran while one was open for 15% of the time, Pallas kernels for 0%

commit v1 on v0

--- a/solution.py
+++ b/solution.py
@@ -1,6 +1,8 @@
 import jax
 import jax.numpy as jnp
 from jax import lax
+from jax.experimental import pallas as pl
+from jax.experimental.pallas import tpu as pltpu
 from jax.sharding import PartitionSpec as P
 
 WINDOW = 7
@@ -229,58 +231,234 @@
     return (grad_resid + back_one, grads, factors)
 
 
-def share_out(grads):
-    return (
-        lax.psum_scatter(
-            grads[0].astype(jnp.bfloat16), "fsdp", scatter_dimension=0, tiled=True
-        ).astype(jnp.float32),
-        lax.psum_scatter(
-            grads[1].astype(jnp.bfloat16), "fsdp", scatter_dimension=0, tiled=True
-        ).astype(jnp.float32),
-        lax.psum_scatter(
-            grads[2].astype(jnp.bfloat16), "fsdp", scatter_dimension=0, tiled=True
-        ).astype(jnp.float32),
-        lax.psum_scatter(
-            grads[3].astype(jnp.bfloat16), "fsdp", scatter_dimension=0, tiled=True
-        ).astype(jnp.float32),
-        lax.psum_scatter(
-            grads[4].astype(jnp.bfloat16), "fsdp", scatter_dimension=0, tiled=True
-        ).astype(jnp.float32),
-        lax.psum_scatter(
-            grads[5].astype(jnp.bfloat16), "fsdp", scatter_dimension=0, tiled=True
-        ).astype(jnp.float32),
-        lax.psum_scatter(
-            grads[6].astype(jnp.bfloat16), "fsdp", scatter_dimension=0, tiled=True
-        ).astype(jnp.float32),
-        lax.psum_scatter(
-            grads[7].astype(jnp.bfloat16), "fsdp", scatter_dimension=0, tiled=True
-        ).astype(jnp.float32),
-        lax.psum_scatter(
-            grads[8].astype(jnp.bfloat16), "fsdp", scatter_dimension=1, tiled=True
-        ).astype(jnp.float32),
-        lax.psum_scatter(
-            grads[9].astype(jnp.bfloat16), "fsdp", scatter_dimension=1, tiled=True
-        ).astype(jnp.float32),
-        lax.psum_scatter(
-            grads[10].astype(jnp.bfloat16), "fsdp", scatter_dimension=1, tiled=True
-        ).astype(jnp.float32),
-    )
-
-
-def sum_groups(shares):
-    return (
-        lax.psum(shares[0].astype(jnp.bfloat16), "dp").astype(jnp.float32),
-        lax.psum(shares[1].astype(jnp.bfloat16), "dp").astype(jnp.float32),
-        lax.psum(shares[2].astype(jnp.bfloat16), "dp").astype(jnp.float32),
-        lax.psum(shares[3].astype(jnp.bfloat16), "dp").astype(jnp.float32),
-        lax.psum(shares[4].astype(jnp.bfloat16), "dp").astype(jnp.float32),
-        lax.psum(shares[5].astype(jnp.bfloat16), "dp").astype(jnp.float32),
-        lax.psum(shares[6].astype(jnp.bfloat16), "dp").astype(jnp.float32),
-        lax.psum(shares[7].astype(jnp.bfloat16), "dp").astype(jnp.float32),
-        lax.psum(shares[8].astype(jnp.bfloat16), "dp").astype(jnp.float32),
-        lax.psum(shares[9].astype(jnp.bfloat16), "dp").astype(jnp.float32),
-        lax.psum(shares[10].astype(jnp.bfloat16), "dp").astype(jnp.float32),
-    )
+FSDP_PAIRS = (
+    [(f, f ^ 4) for f in range(16)],
+    [(f, (3 - f // 4) * 4 + f % 4) for f in range(16)],
+    [(f, f ^ 1) for f in range(16)],
+    [(f, f // 4 * 4 + 3 - f % 4) for f in range(16)],
+)
+X_PAIRS = ([(d, d ^ 2) for d in range(8)], [(d, (3 - d // 2) * 2 + d % 2) for d in range(8)])
+CORE_PAIRS = [(d, d ^ 1) for d in range(8)]
+ORDERS = ((0, 1, 2, 3), (1, 0, 3, 2), (2, 3, 0, 1), (3, 2, 1, 0))
+LANES = 128
+SMALL = 16
+ROWS = 192
+SHARES = 16
+
+
+def group_rows(group):
+    return ROWS + SMALL if group == 0 else ROWS
+
+
+def my_place():
+    share = lax.axis_index("fsdp")
+    core = lax.axis_index("dp") % 2
+    z_at, y_at = share // 4, share % 4
+    z_v, y_v = z_at // 2, y_at // 2
+    bits = [(z_at + z_v) % 2, z_v, (y_at + y_v) % 2, y_v]
+    return jnp.stack(bits + [core]).astype(jnp.int32)
+
+
+def share_at(place, group, slot):
+    bits = [None] * 4
+    for at, bit in enumerate(ORDERS[group]):
+        own = place[bit]
+        bits[bit] = 1 - own if (slot >> (3 - at)) & 1 else own
+    z_low = jnp.where(bits[0] == bits[1], 0, 1)
+    y_low = jnp.where(bits[2] == bits[3], 0, 1)
+    return (bits[1] * 2 + z_low) * 4 + bits[3] * 2 + y_low
+
+
+def chunk_place(chunk, group):
+    at = group * LANES
+    if chunk < 3:
+        return (0, 0, chunk * 512 + at)
+    if chunk == 3:
+        return (1, 0, at)
+    if chunk < 8:
+        return (2, 0, (chunk - 4) * 512 + at)
+    return (3, (chunk - 8) * 32, at)
+
+
+def pack_small(parts):
+    rows = []
+    for part in parts:
+        lead = part.shape[0]
+        width = part.shape[-1]
+        for low in range(0, width, LANES):
+            piece = part[:, low : low + LANES]
+            rows.append(jnp.pad(piece, ((0, 0), (0, LANES - piece.shape[1]))))
+    while len(rows) < SMALL:
+        rows.append(jnp.zeros((lead, LANES), rows[0].dtype))
+    return jnp.stack(rows, 1)
+
+
+def gather_parts(qkv, proj, fc1, fc2, small):
+    core = lax.axis_index("dp") % 2
+    chunks = [qkv[:, 0:512], qkv[:, 512:1024], qkv[:, 1024:], proj]
+    chunks += [fc1[:, at * 512 : at * 512 + 512] for at in range(4)]
+    chunks += [fc2[at * 32 : at * 32 + 32] for at in range(4)]
+    even = jnp.concatenate(chunks[0::2], 0)
+    odd = jnp.concatenate(chunks[1::2], 0)
+    mine = jnp.where(core == 0, even, odd)
+    bufs = []
+    for group in range(4):
+        piece = mine[:, group * LANES : (group + 1) * LANES]
+        if group == 0:
+            piece = jnp.concatenate([piece, small], 0)
+        bufs.append(piece[None])
+    return bufs
+
+
+def gather_over_chips(bufs):
+    firsts, seconds = [], []
+    for step in range(4):
+        for group in range(4):
+            pairs = FSDP_PAIRS[ORDERS[group][3 - step]]
+            other = lax.ppermute(bufs[group], "fsdp", pairs)
+            if step < 3:
+                bufs[group] = jnp.concatenate([bufs[group], other], 0)
+            else:
+                firsts.append(bufs[group])
+                seconds.append(other)
+    operands = []
+    for group in range(4):
+        operands += [
+            firsts[group],
+            seconds[group],
+            lax.ppermute(firsts[group], "dp", CORE_PAIRS),
+            lax.ppermute(seconds[group], "dp", CORE_PAIRS),
+        ]
+    return operands
+
+
+def unpack_body(place, *refs):
+    pieces, outs = refs[:16], refs[16:]
+    first_core = place[4] == 0
+    for group in range(4):
+        for slot in range(16):
+            share = share_at(place, group, slot)
+            own_ref = pieces[group * 4 + slot // 8]
+            other_ref = pieces[group * 4 + 2 + slot // 8]
+            for step in range(6):
+                rows = pl.ds(step * 32, 32)
+                own = own_ref[slot % 8, rows, :]
+                other = other_ref[slot % 8, rows, :]
+                even = jnp.where(first_core, own, other)
+                odd = jnp.where(first_core, other, own)
+                for chunk, value in ((2 * step, even), (2 * step + 1, odd)):
+                    out, row, lane = chunk_place(chunk, group)
+                    outs[out][share, pl.ds(row, 32), pl.ds(lane, LANES)] = value
+            if group == 0:
+                outs[4][share] = own_ref[slot % 8, pl.ds(ROWS, SMALL), :]
+
+
+def unpack_parts(place, operands):
+    dtype = operands[0].dtype
+    shapes = ((32, 1536), (32, 512), (32, 2048), (128, 512), (SMALL, LANES))
+    outs = pl.pallas_call(
+        unpack_body,
+        in_specs=[pl.BlockSpec(memory_space=pltpu.SMEM)]
+        + [pl.BlockSpec(memory_space=pltpu.VMEM)] * 16,
+        out_specs=[pl.BlockSpec(memory_space=pltpu.VMEM)] * 5,
+        out_shape=[jax.ShapeDtypeStruct((SHARES,) + shape, dtype) for shape in shapes],
+        name="unpack_parts",
+    )(place, *operands)
+    return outs
+
+
+def pack_body(place, qkv, proj, fc1, fc2, small, *outs):
+    sources = (qkv, proj, fc1, fc2)
+    first_core = place[4] == 0
+    for group in range(4):
+        for slot in range(16):
+            share = share_at(place, group, slot)
+            for step in range(6):
+                values = []
+                for chunk in (2 * step, 2 * step + 1):
+                    source, row, lane = chunk_place(chunk, group)
+                    values.append(sources[source][share, pl.ds(row, 32), pl.ds(lane, LANES)])
+                own = jnp.where(first_core, values[0], values[1])
+                other = jnp.where(first_core, values[1], values[0])
+                rows = pl.ds(step * 32, 32)
+                outs[group * 2][slot, rows, :] = own
+                outs[group * 2 + 1][slot, rows, :] = other
+            if group == 0:
+                value = small[share]
+                outs[0][slot, pl.ds(ROWS, SMALL), :] = value
+                outs[1][slot, pl.ds(ROWS, SMALL), :] = value
+
+
+def pack_grads(place, qkv, proj, fc1, fc2, small):
+    shapes = [(SHARES, group_rows(group), LANES) for group in range(4) for _ in range(2)]
+    return pl.pallas_call(
+        pack_body,
+        in_specs=[pl.BlockSpec(memory_space=pltpu.SMEM)]
+        + [pl.BlockSpec(memory_space=pltpu.VMEM)] * 5,
+        out_specs=[pl.BlockSpec(memory_space=pltpu.VMEM)] * 8,
+        out_shape=[jax.ShapeDtypeStruct(shape, jnp.bfloat16) for shape in shapes],
+        name="pack_grads",
+    )(place, qkv, proj, fc1, fc2, small)
+
+
+def add_rounded(first, second):
+    return (first.astype(jnp.float32) + second.astype(jnp.float32)).astype(jnp.bfloat16)
+
+
+def reduce_parts(packed):
+    bufs = []
+    for group in range(4):
+        other = lax.ppermute(packed[group * 2 + 1], "dp", CORE_PAIRS)
+        bufs.append(add_rounded(packed[group * 2], other))
+    for step in range(4):
+        half = 8 >> step
+        for group in range(4):
+            pairs = FSDP_PAIRS[ORDERS[group][step]]
+            other = lax.ppermute(bufs[group][half:], "fsdp", pairs)
+            bufs[group] = add_rounded(bufs[group][:half], other)
+    joined = [
+        jnp.concatenate([bufs[0][0], bufs[1][0]], 0),
+        jnp.concatenate([bufs[2][0], bufs[3][0]], 0),
+    ]
+    for step in range(2):
+        for at in range(2):
+            other = lax.ppermute(joined[at], "dp", X_PAIRS[(step + at) % 2])
+            joined[at] = add_rounded(joined[at], other)
+    others = [lax.ppermute(joined[at], "dp", CORE_PAIRS) for at in range(2)]
+    return joined + others
+
+
+def finish_body(place, *refs):
+    parts, outs = refs[: 4 * LAYERS], refs[4 * LAYERS :]
+    first_core = place[4] == 0
+    for layer_id in range(LAYERS):
+        for group in range(4):
+            base = 0 if group % 2 == 0 else group_rows(group - 1)
+            own_ref = parts[layer_id * 4 + group // 2]
+            other_ref = parts[layer_id * 4 + 2 + group // 2]
+            for step in range(6):
+                rows = pl.ds(base + step * 32, 32)
+                own = own_ref[rows, :].astype(jnp.float32)
+                other = other_ref[rows, :].astype(jnp.float32)
+                even = jnp.where(first_core, own, other)
+                odd = jnp.where(first_core, other, own)
+                for chunk, value in ((2 * step, even), (2 * step + 1, odd)):
+                    out, row, lane = chunk_place(chunk, group)
+                    outs[out][layer_id, pl.ds(row, 32), pl.ds(lane, LANES)] = value
+            if group == 0:
+                outs[4][layer_id] = own_ref[pl.ds(ROWS, SMALL), :].astype(jnp.float32)
+
+
+def finish_grads(place, parts):
+    shapes = ((32, 1536), (32, 512), (32, 2048), (128, 512), (SMALL, LANES))
+    return pl.pallas_call(
+        finish_body,
+        in_specs=[pl.BlockSpec(memory_space=pltpu.SMEM)]
+        + [pl.BlockSpec(memory_space=pltpu.VMEM)] * (4 * LAYERS),
+        out_specs=[pl.BlockSpec(memory_space=pltpu.VMEM)] * 5,
+        out_shape=[jax.ShapeDtypeStruct((LAYERS,) + shape, jnp.float32) for shape in shapes],
+        name="finish_grads",
+    )(place, *parts)
 
 
 def on_device(
@@ -312,24 +490,59 @@
         flat_bias = grad_bias.transpose(1, 2, 0).reshape(WIN_TOK * WIN_TOK, -1)
         return jnp.einsum("pr,ph->rh", onehot, flat_bias, precision=lax.Precision.HIGHEST)
 
+    place = my_place()
+    bufs_all = []
+    for layer_id in range(LAYERS):
+        small = pack_small(
+            [
+                qv_bias[layer_id][None],
+                proj_bias[layer_id][None],
+                fc1_bias[layer_id][None],
+                fc2_bias[layer_id][None],
+                norm_gains[layer_id, 0][None],
+                norm_gains[layer_id, 1][None],
+                norm_biases[layer_id, 0][None],
+                norm_biases[layer_id, 1][None],
+                rel_table[layer_id][:, 0][None],
+            ]
+        )[0]
+        bufs_all.append(
+            gather_parts(
+                qkv_weight[layer_id],
+                proj_weight[layer_id],
+                fc1_weight[layer_id],
+                fc2_weight[layer_id],
+                small,
+            )
+        )
+    weights_all = []
+    pos_biases = []
+    operands = None
+    for layer_id in range(LAYERS):
+        bufs = bufs_all[layer_id]
+        if operands is not None:
+            bufs, _ = lax.optimization_barrier((bufs, operands))
+        operands = gather_over_chips(list(bufs))
+        qkv_w, proj_w, fc1_w, fc2_w, small = unpack_parts(place, operands)
+        weights_all.append(
+            (
+                qkv_w.reshape(512, 1536),
+                small[:, 0, :64].reshape(-1),
+                proj_w.reshape(512, 512),
+                small[:, 1, :32].reshape(-1),
+                fc1_w.reshape(512, 2048),
+                small[:, 2].reshape(-1),
+                fc2_w.reshape(2048, 512),
+                small[:, 3, :32].reshape(-1),
+                small[:, 4:6, :32].transpose(1, 0, 2).reshape(2, -1),
+                small[:, 6:8, :32].transpose(1, 0, 2).reshape(2, -1),
+                small[:, 8:10].reshape(SHARES, -1)[:, :TABLE].T,
+            )
+        )
     tokens_f = images.astype(jnp.float32).reshape(-1, feat_dim)
     saved_all = []
-    kept_all = []
-    pos_biases = []
     for layer_id in range(LAYERS):
-        weights = (
-            lax.all_gather(qkv_weight[layer_id], "fsdp", axis=0, tiled=True),
-            lax.all_gather(qv_bias[layer_id], "fsdp", axis=0, tiled=True),
-            lax.all_gather(proj_weight[layer_id], "fsdp", axis=0, tiled=True),
-            lax.all_gather(proj_bias[layer_id], "fsdp", axis=0, tiled=True),
-            lax.all_gather(fc1_weight[layer_id], "fsdp", axis=0, tiled=True),
-            lax.all_gather(fc1_bias[layer_id], "fsdp", axis=0, tiled=True),
-            lax.all_gather(fc2_weight[layer_id], "fsdp", axis=0, tiled=True),
-            lax.all_gather(fc2_bias[layer_id], "fsdp", axis=0, tiled=True),
-            lax.all_gather(norm_gains[layer_id], "fsdp", axis=1, tiled=True),
-            lax.all_gather(norm_biases[layer_id], "fsdp", axis=1, tiled=True),
-            lax.all_gather(rel_table[layer_id], "fsdp", axis=1, tiled=True),
-        )
+        weights = weights_all[layer_id]
         shifted = layer_id % 2 == 1
         gathered = jnp.einsum(
             "pr,rh->ph", onehot, weights[10].astype(jnp.float32), precision=lax.Precision.HIGHEST
@@ -339,55 +552,58 @@
             tokens_f, weights, shifted, pos_bias, allowed if shifted else None
         )
         saved_all.append(saved)
-        kept_all.append(weights)
         pos_biases.append(pos_bias)
     activations = tokens_f.reshape(n_images, TOKENS_IMG, feat_dim) * live_mask
     gradient = (cotangent.astype(jnp.float32) * live_mask).reshape(-1, feat_dim)
-    totals_all = [None] * LAYERS
+    parts_all = [None] * LAYERS
     for layer_id in reversed(range(LAYERS)):
-        weights = (
-            lax.all_gather(qkv_weight[layer_id], "fsdp", axis=0, tiled=True),
-            lax.all_gather(qv_bias[layer_id], "fsdp", axis=0, tiled=True),
-            lax.all_gather(proj_weight[layer_id], "fsdp", axis=0, tiled=True),
-            lax.all_gather(proj_bias[layer_id], "fsdp", axis=0, tiled=True),
-            lax.all_gather(fc1_weight[layer_id], "fsdp", axis=0, tiled=True),
-            lax.all_gather(fc1_bias[layer_id], "fsdp", axis=0, tiled=True),
-            lax.all_gather(fc2_weight[layer_id], "fsdp", axis=0, tiled=True),
-            lax.all_gather(fc2_bias[layer_id], "fsdp", axis=0, tiled=True),
-            lax.all_gather(norm_gains[layer_id], "fsdp", axis=1, tiled=True),
-            lax.all_gather(norm_biases[layer_id], "fsdp", axis=1, tiled=True),
-            lax.all_gather(rel_table[layer_id], "fsdp", axis=1, tiled=True),
-        )
         shifted = layer_id % 2 == 1
         gradient, grads, factors = layer_backward(
             gradient,
             saved_all[layer_id],
-            weights,
+            weights_all[layer_id],
             shifted,
             pos_biases[layer_id],
             allowed if shifted else None,
             fold_bias,
         )
-        shares = share_out(grads)
-        totals_all[layer_id] = sum_groups(shares)
-    stacked = [
-        jnp.stack([totals_all[layer_id][member] for layer_id in range(LAYERS)])
-        for member in range(11)
-    ]
+        small = pack_small(
+            [
+                grads[1].reshape(SHARES, -1),
+                grads[3].reshape(SHARES, -1),
+                grads[5].reshape(SHARES, -1),
+                grads[7].reshape(SHARES, -1),
+                grads[8][0].reshape(SHARES, -1),
+                grads[8][1].reshape(SHARES, -1),
+                grads[9][0].reshape(SHARES, -1),
+                grads[9][1].reshape(SHARES, -1),
+                grads[10].T,
+            ]
+        ).astype(jnp.bfloat16)
+        packed = pack_grads(
+            place,
+            grads[0].astype(jnp.bfloat16).reshape(SHARES, 32, -1),
+            grads[2].astype(jnp.bfloat16).reshape(SHARES, 32, -1),
+            grads[4].astype(jnp.bfloat16).reshape(SHARES, 32, -1),
+            grads[6].astype(jnp.bfloat16).reshape(SHARES, 128, -1),
+            small,
+        )
+        parts_all[layer_id] = reduce_parts(packed)
+    qkv_g, proj_g, fc1_g, fc2_g, small = finish_grads(place, sum(parts_all, []))
     return (
         activations,
         gradient.reshape(n_images, TOKENS_IMG, feat_dim),
-        stacked[0],
-        stacked[1],
-        stacked[2],
-        stacked[3],
-        stacked[4],
-        stacked[5],
-        stacked[6],
-        stacked[7],
-        stacked[8],
-        stacked[9],
-        stacked[10],
+        qkv_g,
+        small[:, 0, :64],
+        proj_g,
+        small[:, 1, :32],
+        fc1_g,
+        small[:, 2],
+        fc2_g,
+        small[:, 3, :32],
+        small[:, 4:6, :32],
+        small[:, 6:8, :32],
+        small[:, 8:10].reshape(LAYERS, -1)[:, :TABLE, None],
     )
 
 

time: 1610 us -> 544 us (0.34)
  waiting for transfers between devices: 865 us -> 78.3 us
  blocking collectives: 334 us -> 0 us
  starting transfers between devices: 1.28 us -> 105 us
  Pallas kernels: 0 us -> 30.3 us
  matrix products: 109 us -> 82.9 us
  local copies, waits for them, and re-layouts: 211 us -> 187 us
    reduce_scatter x8 -> x0, waiting for transfers between devices: 613 us -> none  [the longest x2 156 us: share_out(): lax.psum_scatter(grads[4].astype(jnp.bfloat16), 'fsdp', scatter_dimension...]
    all_gather x10 -> x0, blocking collectives: 219 us -> none  [the longest x2 47.4 us: on_device(): lax.all_gather(proj_weight[layer_id], 'fsdp', axis=0, tiled=True)]
    unnamed x24 -> x0, waiting for transfers between devices: 167 us -> none
    unnamed x2 -> x0, blocking collectives: 115 us -> none
    ppermute x0 -> x100, starting transfers between devices: none -> 105 us  [the longest x32 51.6 us: gather_over_chips(): other = lax.ppermute(bufs[group], 'fsdp', pairs)]
    psum x2 -> x0, waiting for transfers between devices: 85.2 us -> none  [the longest x1 58.5 us: sum_groups(): lax.psum(shares[0].astype(jnp.bfloat16), 'dp').astype(jnp.float32)]
    ppermute x0 -> x100, waiting for transfers between devices: none -> 78.3 us  [the longest x32 37.2 us: gather_over_chips(): other = lax.ppermute(bufs[group], 'fsdp', pairs)]
    pallas_call x0 -> x5, Pallas kernels: none -> 30.3 us  [the longest x2 14.4 us: pack_grads(): pl.pallas_call(pack_body, in_specs=[pl.BlockSpec(memory_space=pltpu.SMEM)...]
  transfers between devices with their start and end apart: 20 -> 100, of which waited for: 13 -> 32; matrix products, arithmetic and copies ran while one was open for 15% -> 9% of each run, Pallas kernels for 0% -> 3%
where the time goes in v1:
time: 544 us; the launch traced here: 538 us
  local copies, waits for them, and re-layouts  187 us (34%)
  starting transfers between devices  105 us (19%)
  matrix products  82.9 us (15%)
  waiting for transfers between devices  78.3 us (14%)
  other arithmetic  49 us (9%)
  Pallas kernels  30.3 us (6%)
    dot_general x36, matrix products, product(): jnp.einsum(pattern, first_op, second_op, preferred_element_type=jnp.float32)  79.2 us
    ppermute x32, starting transfers between devices, gather_over_chips(): other = lax.ppermute(bufs[group], 'fsdp', pairs)  51.6 us
    another operation x16, local copies, waits for them, and re-layouts, split_heads(): return windows.reshape(windows.shape[0], WIN_TOK, n_heads, -1)  44.6 us
    ppermute x32, waiting for transfers between devices, gather_over_chips(): other = lax.ppermute(bufs[group], 'fsdp', pairs)  37.2 us
    ppermute x32, starting transfers between devices, reduce_parts(): other = lax.ppermute(bufs[group][half:], 'fsdp', pairs)  37.1 us
    ppermute x32, waiting for transfers between devices, reduce_parts(): other = lax.ppermute(bufs[group][half:], 'fsdp', pairs)  29.5 us
    unnamed x312, local copies, waits for them, and re-layouts  23.7 us
    another operation x7, local copies, waits for them, and re-layouts, from_windows(): windows.reshape(n_images, per_side, per_side, WINDOW, WINDOW, channels)  21.9 us
  transfers between devices with their start and end apart: 100, of which 32 were waited for; matrix products, arithmetic and copies ran while one was open for 9% of the time, Pallas kernels for 3%

profile of v1, /device:TPU:0, one launch (start us, length us, event | category | flops | bytes accessed | tf_op | source)
XLA Modules:
  0.0 537.8 jit_solution(11390337429571432551)
XLA Ops:
  17.0 4.7 collective-permute-done.7
  31.6 13.2 %collective-permute-done.2 = bf16[4,208,128]{2,1,0:T(8,128)(2,1)S(1)} collective-permute-done((bf16[4,208,128]{2,1,0:T(8,128)(2,1)S(1)}, bf16[4,208,128]{2,1,0:T(8,128)(2,1)S(1)}, u32[]{:S(2)}, u32[]{:S(2)}) %collective-permute-start.2) | collective-permute-done | bytes 213024 | tf_op jit(solution)/shard_map/ppermute | solution.py:318
  48.3 9.5 %collective-permute-done.21.refs_13_ = bf16[8,192,128]{2,1,0:T(8,128)(2,1)} collective-permute-done((bf16[8,192,128]{2,1,0:T(8,128)(2,1)S(1)}, bf16[8,192,128]{2,1,0:T(8,128)(2,1)}, u32[]{:S(2)}, u32[]{:S(2)}) %collective-permute-start.21) | collective-permute-done | bytes 393248 | tf_op jit(solution)/shard_map/ppermute | solution.py:318
  69.4 11.1 %collective-permute-start.42 = (bf16[1,192,128]{2,1,0:T(8,128)(2,1)S(1)}, bf16[1,192,128]{2,1,0:T(8,128)(2,1)S(1)}, u32[]{:S(2)}, u32[]{:S(2)}) collective-permute-start(bf16[1,192,128]{2,1,0:T(8,128)(2,1)S(1)} %get-tuple-element.56), channel_id=1, source_target_pairs={{0,4},{1,5},{2,6},{3,7},{4,0},{5,1},{6,2},{7,3},{8,12},{9,13},{10,... | collective-permute-start | bytes 147464 | tf_op jit(solution)/shard_map/ppermute | solution.py:318
  80.5 6.7 %unpack_parts.2 = (bf16[16,32,1536]{2,1,0:T(8,128)(2,1)}, bf16[16,32,512]{2,1,0:T(8,128)(2,1)}, bf16[16,32,2048]{2,1,0:T(8,128)(2,1)}, bf16[16,128,512]{2,1,0:T(8,128)(2,1)}, bf16[16,16,128]{2,1,0:T(8,128)(2,1)}) custom-call(s32[5]{0:T(128)} %stack.177.place, bf16[8,208,128]{2,1,0:T(8,128)(2,1)} %copy-done.31, ...), custom_call_target="tpu_custom_call" | custom-call | tf_op jit(solution)/shard_map/unpack_parts/pallas_call | solution.py:359
  112.2 5.7 %collective-permute-done.45.refs_13_ = bf16[8,192,128]{2,1,0:T(8,128)(2,1)S(1)} collective-permute-done((bf16[8,192,128]{2,1,0:T(8,128)(2,1)S(1)}, bf16[8,192,128]{2,1,0:T(8,128)(2,1)S(1)}, u32[]{:S(2)}, u32[]{:S(2)}) %collective-permute-start.45) | collective-permute-done | bytes 393248 | tf_op jit(solution)/shard_map/ppermute | solution.py:318
  129.6 3.7 copy.321
  137.7 6.8 %unpack_parts.3 = (bf16[16,32,1536]{2,1,0:T(8,128)(2,1)}, bf16[16,32,512]{2,1,0:T(8,128)(2,1)}, bf16[16,32,2048]{2,1,0:T(8,128)(2,1)}, bf16[16,128,512]{2,1,0:T(8,128)(2,1)}, bf16[16,16,128]{2,1,0:T(8,128)(2,1)}) custom-call(s32[5]{0:T(128)} %stack.177.place, bf16[8,208,128]{2,1,0:T(8,128)(2,1)} %constant_dynamic-update-slice_fusion.24.refs_0_, ...), custom_call_target="tpu_custom_call" | custom-call | tf_op jit(solution)/shard_map/unpack_parts/pallas_call | solution.py:359
  160.3 3.7 copy.320
  170.2 3.9 copy.325
  201.3 3.6 reshape_reshape.80
  204.9 3.7 copy.334
  210.6 3.9 copy.337
  221.1 3.9 copy.339
  243.7 5.2 fusion.110
  255.6 4.4 convolution_convert_fusion
  269.6 3.7 copy.345
  273.3 4.8 convolution_bitcast_fusion
  278.1 5.0 copy.359
  298.7 4.6 copy.354
  309.0 4.9 copy.349
  348.4 3.6 multiply_reduce_fusion
  360.8 4.6 copy.367
  365.3 3.6 reshape_reshape.93
  370.9 4.6 copy.375
  375.5 3.6 reshape_reshape.95
  381.1 4.7 copy.371
  404.2 7.2 %pack_grads.3 = (bf16[16,208,128]{2,1,0:T(8,128)(2,1)}, bf16[16,208,128]{2,1,0:T(8,128)(2,1)}, bf16[16,192,128]{2,1,0:T(8,128)(2,1)}, bf16[16,192,128]{2,1,0:T(8...) custom-call(s32[5]{0:T(128)} %stack.177.place, ...), custom_call_target="tpu_custom_call" | custom-call | tf_op jit(solution)/shard_map/pack_grads/pallas_call | solution.py:394
  420.0 7.2 %pack_grads.2 = (bf16[16,208,128]{2,1,0:T(8,128)(2,1)}, bf16[16,208,128]{2,1,0:T(8,128)(2,1)}, bf16[16,192,128]{2,1,0:T(8,128)(2,1)}, bf16[16,192,128]{2,1,0:T(8...) custom-call(s32[5]{0:T(128)} %stack.177.place, ...), custom_call_target="tpu_custom_call" | custom-call | tf_op jit(solution)/shard_map/pack_grads/pallas_call | solution.py:394
  441.6 4.5 collective-permute-done.80
  450.2 3.6 collective-permute-done.54
  460.8 8.8 %collective-permute-done.49 = bf16[8,208,128]{2,1,0:T(8,128)(2,1)S(1)} collective-permute-done((bf16[8,208,128]{2,1,0:T(8,128)(2,1)S(1)}, bf16[8,208,128]{2,1,0:T(8,128)(2,1)S(1)}, u32[]{:S(2)}, u32[]{:S(2)}) %collective-permute-start.49) | collective-permute-done | bytes 426016 | tf_op jit(solution)/shard_map/ppermute | solution.py:417
  (944 shorter events, 359.8 us)
Async XLA Ops:
  27.4 17.5 %collective-permute-start.10 = (bf16[8,192,128]{2,1,0:T(8,128)(2,1)S(1)}, bf16[8,192,128]{2,1,0:T(8,128)(2,1)S(1)}, u32[]{:S(2)}, u32[]{:S(2)}) collective-permute-start(bf16[8,192,128]{2,1,0:T(8,128)(2,1)S(1)} %pad_maximum_fusion.13.refs_4_), channel_id=1, source_target_pairs={{0,16},{16,0},{32,48},{48,32},{64,80},{80,64},{96,112},{112,96},{1... | collective-permute-start | bytes 1179656 | tf_op jit(solution)/shard_map/ppermute | solution.py:329
  27.5 18.5 %collective-permute-start.9 = (bf16[8,192,128]{2,1,0:T(8,128)(2,1)S(1)}, bf16[8,192,128]{2,1,0:T(8,128)(2,1)}, u32[]{:S(2)}, u32[]{:S(2)}) collective-permute-start(bf16[8,192,128]{2,1,0:T(8,128)(2,1)S(1)} %pad_maximum_fusion.13.refs_4_), channel_id=1, source_target_pairs={{0,12},{1,13},{2,14},{3,15},{4,8},{5,9},{6,10},{7,11},{8,4},{9,5},... | collective-permute-start | bytes 1179656 | tf_op jit(solution)/shard_map/ppermute | solution.py:318
  30.3 14.6 %collective-permute-start.2 = (bf16[4,208,128]{2,1,0:T(8,128)(2,1)S(1)}, bf16[4,208,128]{2,1,0:T(8,128)(2,1)S(1)}, u32[]{:S(2)}, u32[]{:S(2)}) collective-permute-start(bf16[4,208,128]{2,1,0:T(8,128)(2,1)S(1)} %pad_maximum_fusion.16), channel_id=1, source_target_pairs={{0,12},{1,13},{2,14},{3,15},{4,8},{5,9},{6,10},{7,11},{8,4},{9,5},... | collective-permute-start | bytes 638984 | tf_op jit(solution)/shard_map/ppermute | solution.py:318
  31.1 16.6 %collective-permute-start.16 = (bf16[8,192,128]{2,1,0:T(8,128)(2,1)S(1)}, bf16[8,192,128]{2,1,0:T(8,128)(2,1)S(1)}, u32[]{:S(2)}, u32[]{:S(2)}) collective-permute-start(bf16[8,192,128]{2,1,0:T(8,128)(2,1)S(1)} %pad_maximum_fusion.14.refs_8_), channel_id=1, source_target_pairs={{0,16},{16,0},{32,48},{48,32},{64,80},{80,64},{96,112},{112,96},{1... | collective-permute-start | bytes 1179656 | tf_op jit(solution)/shard_map/ppermute | solution.py:329
  31.2 16.6 %collective-permute-start.15 = (bf16[8,192,128]{2,1,0:T(8,128)(2,1)S(1)}, bf16[8,192,128]{2,1,0:T(8,128)(2,1)}, u32[]{:S(2)}, u32[]{:S(2)}) collective-permute-start(bf16[8,192,128]{2,1,0:T(8,128)(2,1)S(1)} %pad_maximum_fusion.14.refs_8_), channel_id=1, source_target_pairs={{0,1},{1,0},{2,3},{3,2},{4,5},{5,4},{6,7},{7,6},{8,9},{9,8},{10,11... | collective-permute-start | bytes 1179656 | tf_op jit(solution)/shard_map/ppermute | solution.py:318
  47.6 15.2 %collective-permute-start.4 = (bf16[8,208,128]{2,1,0:T(8,128)(2,1)S(1)}, bf16[8,208,128]{2,1,0:T(8,128)(2,1)}, u32[]{:S(2)}, u32[]{:S(2)}) collective-permute-start(bf16[8,208,128]{2,1,0:T(8,128)(2,1)S(1)} %pad_maximum_fusion.9.refs_0_), channel_id=1, source_target_pairs={{0,16},{16,0},{32,48},{48,32},{64,80},{80,64},{96,112},{112,96},{1... | collective-permute-start | bytes 1277960 | tf_op jit(solution)/shard_map/ppermute | solution.py:329
  47.7 15.1 %collective-permute-start.11 = (bf16[8,192,128]{2,1,0:T(8,128)(2,1)}, bf16[8,192,128]{2,1,0:T(8,128)(2,1)}, u32[]{:S(2)}, u32[]{:S(2)}) collective-permute-start(bf16[8,192,128]{2,1,0:T(8,128)(2,1)} %collective-permute-done.9.refs_5_), channel_id=1, source_target_pairs={{0,16},{16,0},{32,48},{48,32},{64,80},{80,64},{96,112},{112,96},{1... | collective-permute-start | bytes 1179656 | tf_op jit(solution)/shard_map/ppermute | solution.py:330
  48.2 14.6 %collective-permute-start.17 = (bf16[8,192,128]{2,1,0:T(8,128)(2,1)}, bf16[8,192,128]{2,1,0:T(8,128)(2,1)}, u32[]{:S(2)}, u32[]{:S(2)}) collective-permute-start(bf16[8,192,128]{2,1,0:T(8,128)(2,1)} %collective-permute-done.15.refs_9_), channel_id=1, source_target_pairs={{0,16},{16,0},{32,48},{48,32},{64,80},{80,64},{96,112},{112,96},{1... | collective-permute-start | bytes 1179656 | tf_op jit(solution)/shard_map/ppermute | solution.py:330
  62.8 27.0 %collective-permute-start.30 = (bf16[1,192,128]{2,1,0:T(8,128)(2,1)S(1)}, bf16[1,192,128]{2,1,0:T(8,128)(2,1)S(1)}, u32[]{:S(2)}, u32[]{:S(2)}) collective-permute-start(bf16[1,192,128]{2,1,0:T(8,128)(2,1)S(1)} %get-tuple-element.54), channel_id=1, source_target_pairs={{0,1},{1,0},{2,3},{3,2},{4,5},{5,4},{6,7},{7,6},{8,9},{9,8},{10,11... | collective-permute-start | bytes 147464 | tf_op jit(solution)/shard_map/ppermute | solution.py:318
  63.6 27.6 %collective-permute-start.36 = (bf16[1,192,128]{2,1,0:T(8,128)(2,1)S(1)}, bf16[1,192,128]{2,1,0:T(8,128)(2,1)S(1)}, u32[]{:S(2)}, u32[]{:S(2)}) collective-permute-start(bf16[1,192,128]{2,1,0:T(8,128)(2,1)S(1)} %get-tuple-element.55), channel_id=1, source_target_pairs={{0,12},{1,13},{2,14},{3,15},{4,8},{5,9},{6,10},{7,11},{8,4},{9,5},... | collective-permute-start | bytes 147464 | tf_op jit(solution)/shard_map/ppermute | solution.py:318
  66.8 28.5 %collective-permute-start.24 = (bf16[1,208,128]{2,1,0:T(8,128)(2,1)S(1)}, bf16[1,208,128]{2,1,0:T(8,128)(2,1)S(1)}, u32[]{:S(2)}, u32[]{:S(2)}) collective-permute-start(bf16[1,208,128]{2,1,0:T(8,128)(2,1)S(1)} %maximum_bitcast_fusion.1), channel_id=1, source_target_pairs={{0,3},{1,2},{2,1},{3,0},{4,7},{5,6},{6,5},{7,4},{8,11},{9,10},{10,... | collective-permute-start | bytes 159752 | tf_op jit(solution)/shard_map/ppermute | solution.py:318
  69.4 23.9 %collective-permute-start.42 = (bf16[1,192,128]{2,1,0:T(8,128)(2,1)S(1)}, bf16[1,192,128]{2,1,0:T(8,128)(2,1)S(1)}, u32[]{:S(2)}, u32[]{:S(2)}) collective-permute-start(bf16[1,192,128]{2,1,0:T(8,128)(2,1)S(1)} %get-tuple-element.56), channel_id=1, source_target_pairs={{0,4},{1,5},{2,6},{3,7},{4,0},{5,1},{6,2},{7,3},{8,12},{9,13},{10,... | collective-permute-start | bytes 147464 | tf_op jit(solution)/shard_map/ppermute | solution.py:318
  108.6 24.7 %collective-permute-start.40 = (bf16[8,192,128]{2,1,0:T(8,128)(2,1)}, bf16[8,192,128]{2,1,0:T(8,128)(2,1)}, u32[]{:S(2)}, u32[]{:S(2)}) collective-permute-start(bf16[8,192,128]{2,1,0:T(8,128)(2,1)} %constant_dynamic-update-slice_fusion.32.refs_8_), channel_id=1, source_target_pairs={{0,16},{16,0},{32,48},{48,32},{64,80},{80,64},{96,112},{112,96},{1... | collective-permute-start | bytes 1179656 | tf_op jit(solution)/shard_map/ppermute | solution.py:329
  108.8 24.6 %collective-permute-start.39 = (bf16[8,192,128]{2,1,0:T(8,128)(2,1)}, bf16[8,192,128]{2,1,0:T(8,128)(2,1)}, u32[]{:S(2)}, u32[]{:S(2)}) collective-permute-start(bf16[8,192,128]{2,1,0:T(8,128)(2,1)} %constant_dynamic-update-slice_fusion.32.refs_8_), channel_id=1, source_target_pairs={{0,1},{1,0},{2,3},{3,2},{4,5},{5,4},{6,7},{7,6},{8,9},{9,8},{10,11... | collective-permute-start | bytes 1179656 | tf_op jit(solution)/shard_map/ppermute | solution.py:318
  109.6 24.2 %collective-permute-start.34 = (bf16[8,192,128]{2,1,0:T(8,128)(2,1)}, bf16[8,192,128]{2,1,0:T(8,128)(2,1)}, u32[]{:S(2)}, u32[]{:S(2)}) collective-permute-start(bf16[8,192,128]{2,1,0:T(8,128)(2,1)} %constant_dynamic-update-slice_fusion.28.refs_4_), channel_id=1, source_target_pairs={{0,16},{16,0},{32,48},{48,32},{64,80},{80,64},{96,112},{112,96},{1... | collective-permute-start | bytes 1179656 | tf_op jit(solution)/shard_map/ppermute | solution.py:329
  110.5 23.4 %collective-permute-start.33 = (bf16[8,192,128]{2,1,0:T(8,128)(2,1)}, bf16[8,192,128]{2,1,0:T(8,128)(2,1)}, u32[]{:S(2)}, u32[]{:S(2)}) collective-permute-start(bf16[8,192,128]{2,1,0:T(8,128)(2,1)} %constant_dynamic-update-slice_fusion.28.refs_4_), channel_id=1, source_target_pairs={{0,12},{1,13},{2,14},{3,15},{4,8},{5,9},{6,10},{7,11},{8,4},{9,5},... | collective-permute-start | bytes 1179656 | tf_op jit(solution)/shard_map/ppermute | solution.py:318
  117.9 16.5 %collective-permute-start.27 = (bf16[8,208,128]{2,1,0:T(8,128)(2,1)}, bf16[8,208,128]{2,1,0:T(8,128)(2,1)}, u32[]{:S(2)}, u32[]{:S(2)}) collective-permute-start(bf16[8,208,128]{2,1,0:T(8,128)(2,1)} %constant_dynamic-update-slice_fusion.24.refs_0_), channel_id=1, source_target_pairs={{0,4},{1,5},{2,6},{3,7},{4,0},{5,1},{6,2},{7,3},{8,12},{9,13},{10,... | collective-permute-start | bytes 1277960 | tf_op jit(solution)/shard_map/ppermute | solution.py:318
  411.4 16.0 %collective-permute-start.79 = (bf16[16,192,128]{2,1,0:T(8,128)(2,1)}, bf16[16,192,128]{2,1,0:T(8,128)(2,1)}, u32[]{:S(2)}, u32[]{:S(2)}) collective-permute-start(bf16[16,192,128]{2,1,0:T(8,128)(2,1)} %get-tuple-element.73), channel_id=1, source_target_pairs={{0,16},{16,0},{32,48},{48,32},{64,80},{80,64},{96,112},{112,96},{1... | collective-permute-start | bytes 2359304 | tf_op jit(solution)/shard_map/ppermute | solution.py:411
  411.5 17.8 %collective-permute-start.86 = (bf16[16,192,128]{2,1,0:T(8,128)(2,1)}, bf16[16,192,128]{2,1,0:T(8,128)(2,1)}, u32[]{:S(2)}, u32[]{:S(2)}) collective-permute-start(bf16[16,192,128]{2,1,0:T(8,128)(2,1)} %get-tuple-element.75), channel_id=1, source_target_pairs={{0,16},{16,0},{32,48},{48,32},{64,80},{80,64},{96,112},{112,96},{1... | collective-permute-start | bytes 2359304 | tf_op jit(solution)/shard_map/ppermute | solution.py:411
  411.9 19.1 %collective-permute-start.91 = (bf16[16,192,128]{2,1,0:T(8,128)(2,1)}, bf16[16,192,128]{2,1,0:T(8,128)(2,1)}, u32[]{:S(2)}, u32[]{:S(2)}) collective-permute-start(bf16[16,192,128]{2,1,0:T(8,128)(2,1)} %get-tuple-element.77), channel_id=1, source_target_pairs={{0,16},{16,0},{32,48},{48,32},{64,80},{80,64},{96,112},{112,96},{1... | collective-permute-start | bytes 2359304 | tf_op jit(solution)/shard_map/ppermute | solution.py:411
  412.0 25.6 %collective-permute-start.74 = (bf16[16,208,128]{2,1,0:T(8,128)(2,1)}, bf16[16,208,128]{2,1,0:T(8,128)(2,1)}, u32[]{:S(2)}, u32[]{:S(2)}) collective-permute-start(bf16[16,208,128]{2,1,0:T(8,128)(2,1)} %get-tuple-element.71), channel_id=1, source_target_pairs={{0,16},{16,0},{32,48},{48,32},{64,80},{80,64},{96,112},{112,96},{1... | collective-permute-start | bytes 2555912 | tf_op jit(solution)/shard_map/ppermute | solution.py:411
  437.7 16.1 %collective-permute-start.54 = (bf16[8,192,128]{2,1,0:T(8,128)(2,1)S(1)}, bf16[8,192,128]{2,1,0:T(8,128)(2,1)S(1)}, u32[]{:S(2)}, u32[]{:S(2)}) collective-permute-start(bf16[8,192,128]{2,1,0:T(8,128)(2,1)S(1)} %slice.967), channel_id=1, source_target_pairs={{0,12},{1,13},{2,14},{3,15},{4,8},{5,9},{6,10},{7,11},{8,4},{9,5},... | collective-permute-start | bytes 1179656 | tf_op jit(solution)/shard_map/ppermute | solution.py:417
  439.8 15.4 %collective-permute-start.61 = (bf16[8,192,128]{2,1,0:T(8,128)(2,1)S(1)}, bf16[8,192,128]{2,1,0:T(8,128)(2,1)S(1)}, u32[]{:S(2)}, u32[]{:S(2)}) collective-permute-start(bf16[8,192,128]{2,1,0:T(8,128)(2,1)S(1)} %slice.975), channel_id=1, source_target_pairs={{0,1},{1,0},{2,3},{3,2},{4,5},{5,4},{6,7},{7,6},{8,9},{9,8},{10,11... | collective-permute-start | bytes 1179656 | tf_op jit(solution)/shard_map/ppermute | solution.py:417
  448.4 21.2 %collective-permute-start.49 = (bf16[8,208,128]{2,1,0:T(8,128)(2,1)S(1)}, bf16[8,208,128]{2,1,0:T(8,128)(2,1)S(1)}, u32[]{:S(2)}, u32[]{:S(2)}) collective-permute-start(bf16[8,208,128]{2,1,0:T(8,128)(2,1)S(1)} %slice.959), channel_id=1, source_target_pairs={{0,4},{1,5},{2,6},{3,7},{4,0},{5,1},{6,2},{7,3},{8,12},{9,13},{10,... | collective-permute-start | bytes 1277960 | tf_op jit(solution)/shard_map/ppermute | solution.py:417
  453.8 19.4 %collective-permute-start.81 = (bf16[4,192,128]{2,1,0:T(8,128)(2,1)S(1)}, bf16[4,192,128]{2,1,0:T(8,128)(2,1)S(1)}, u32[]{:S(2)}, u32[]{:S(2)}) collective-permute-start(bf16[4,192,128]{2,1,0:T(8,128)(2,1)S(1)} %slice.1003), channel_id=1, source_target_pairs={{0,4},{1,5},{2,6},{3,7},{4,0},{5,1},{6,2},{7,3},{8,12},{9,13},{10,... | collective-permute-start | bytes 589832 | tf_op jit(solution)/shard_map/ppermute | solution.py:417
  455.3 18.7 %collective-permute-start.88 = (bf16[4,192,128]{2,1,0:T(8,128)(2,1)S(1)}, bf16[4,192,128]{2,1,0:T(8,128)(2,1)S(1)}, u32[]{:S(2)}, u32[]{:S(2)}) collective-permute-start(bf16[4,192,128]{2,1,0:T(8,128)(2,1)S(1)} %slice.1011), channel_id=1, source_target_pairs={{0,3},{1,2},{2,1},{3,0},{4,7},{5,6},{6,5},{7,4},{8,11},{9,10},{10,... | collective-permute-start | bytes 589832 | tf_op jit(solution)/shard_map/ppermute | solution.py:417
  457.0 19.1 %collective-permute-start.93 = (bf16[4,192,128]{2,1,0:T(8,128)(2,1)S(1)}, bf16[4,192,128]{2,1,0:T(8,128)(2,1)S(1)}, u32[]{:S(2)}, u32[]{:S(2)}) collective-permute-start(bf16[4,192,128]{2,1,0:T(8,128)(2,1)S(1)} %slice.1019), channel_id=1, source_target_pairs={{0,1},{1,0},{2,3},{3,2},{4,5},{5,4},{6,7},{7,6},{8,9},{9,8},{10,11... | collective-permute-start | bytes 589832 | tf_op jit(solution)/shard_map/ppermute | solution.py:417
  460.5 17.1 %collective-permute-start.55 = (bf16[4,192,128]{2,1,0:T(8,128)(2,1)S(1)}, bf16[4,192,128]{2,1,0:T(8,128)(2,1)S(1)}, u32[]{:S(2)}, u32[]{:S(2)}) collective-permute-start(bf16[4,192,128]{2,1,0:T(8,128)(2,1)S(1)} %slice.969), channel_id=1, source_target_pairs={{0,4},{1,5},{2,6},{3,7},{4,0},{5,1},{6,2},{7,3},{8,12},{9,13},{10,... | collective-permute-start | bytes 589832 | tf_op jit(solution)/shard_map/ppermute | solution.py:417
  474.0 19.1 %collective-permute-start.76 = (bf16[4,208,128]{2,1,0:T(8,128)(2,1)S(1)}, bf16[4,208,128]{2,1,0:T(8,128)(2,1)S(1)}, u32[]{:S(2)}, u32[]{:S(2)}) collective-permute-start(bf16[4,208,128]{2,1,0:T(8,128)(2,1)S(1)} %slice.995), channel_id=1, source_target_pairs={{0,12},{1,13},{2,14},{3,15},{4,8},{5,9},{6,10},{7,11},{8,4},{9,5},... | collective-permute-start | bytes 638984 | tf_op jit(solution)/shard_map/ppermute | solution.py:417
  476.1 18.2 %collective-permute-start.50 = (bf16[4,208,128]{2,1,0:T(8,128)(2,1)S(1)}, bf16[4,208,128]{2,1,0:T(8,128)(2,1)S(1)}, u32[]{:S(2)}, u32[]{:S(2)}) collective-permute-start(bf16[4,208,128]{2,1,0:T(8,128)(2,1)S(1)} %slice.961), channel_id=1, source_target_pairs={{0,12},{1,13},{2,14},{3,15},{4,8},{5,9},{6,10},{7,11},{8,4},{9,5},... | collective-permute-start | bytes 638984 | tf_op jit(solution)/shard_map/ppermute | solution.py:417
  489.5 14.1 %collective-permute-start.83 = (bf16[1,192,128]{2,1,0:T(8,128)(2,1)S(1)}, bf16[1,192,128]{2,1,0:T(8,128)(2,1)S(1)}, u32[]{:S(2)}, u32[]{:S(2)}) collective-permute-start(bf16[1,192,128]{2,1,0:T(8,128)(2,1)S(1)} %slice.1007), channel_id=1, source_target_pairs={{0,1},{1,0},{2,3},{3,2},{4,5},{5,4},{6,7},{7,6},{8,9},{9,8},{10,11... | collective-permute-start | bytes 147464 | tf_op jit(solution)/shard_map/ppermute | solution.py:417
  512.6 14.7 %collective-permute-start.99 = (bf16[384,128]{1,0:T(8,128)(2,1)S(1)}, bf16[384,128]{1,0:T(8,128)(2,1)S(1)}, u32[]{:S(2)}, u32[]{:S(2)}) collective-permute-start(bf16[384,128]{1,0:T(8,128)(2,1)S(1)} %add_convert_fusion.36.refs_5_), channel_id=1, source_target_pairs={{0,16},{16,0},{32,48},{48,32},{64,80},{80,64},{96,112},{112,96},{1... | collective-permute-start | bytes 294920 | tf_op jit(solution)/shard_map/ppermute | solution.py:427
  (208 other events, 1501.6 us)
